TPU v7x, 32 devices: a whole 2x2x4 slice. The times are simulated.
32 devices in a mesh: group: 2 (over core), dp: 4 (over z), section: 2 (over x), tensor: 2 (over y).
Axes of the slice: x: 2, y: 2, z: 4, core: 2. Of those that a mesh axis runs over, the one named last changes fastest.
Arguments:
- merged: bfloat16 [768, 5120], P('dp'), may hold values from -6 to 6
- counts: int32 [8], P('dp'), may hold values from 4 to 384
- owners: int32 [768, 1], P('dp'), may hold values from 0 to 3; in each aligned block of 192 rows (0 to 191, 192 to 383, ...) at most 96 rows name the same one
- w_merge: bfloat16 [5120, 8192], P(None, ('group', 'section', 'tensor')), may hold values from -0.078125 to 0.078125
- norm_gain: float32 [8192], P(('group', 'section', 'tensor')), may hold values from 0.25 to 1.75
- cotangent: bfloat16 [4, 4, 96, 8192], P('dp', None, None, ('group', 'section', 'tensor')), may hold values from -6 to 6
Outputs:
- embedded: bfloat16 [4, 4, 96, 8192], P('dp', None, None, ('group', 'section', 'tensor'))
- grad_merged: float32 [768, 5120], P('dp', ('group', 'section', 'tensor'))
- grad_weight: float32 [5120, 8192], P('dp', ('group', 'section', 'tensor'))
Inputs may be any that keep to these rules, and one draw needn't show every extreme that they name: `owners`: in each replica's 192 rows no owner appears more than 96 times.
All inputs are finite; a program needn't handle non-finite values.
Results may differ from a plain program's by a relative error of at most 0.0049.
Values may be sent and summed in bfloat16 or wider, within the bound.
A program may use at most 64 MiB of HBM per device.

v0:
```python
import jax
import jax.numpy as jnp
from jax import lax
from jax.sharding import PartitionSpec as P

D = 8192


def on_device(merged, counts, owners, w_merge, norm_gain, cotangent):
    rows = merged.shape[0]
    columns = w_merge.shape[1]
    replicas = lax.axis_size("dp")
    slots = cotangent.shape[2]
    images = counts.shape[0]
    per_image = rows // images
    projected = jnp.dot(merged, w_merge, preferred_element_type=jnp.float32).astype(jnp.bfloat16)
    row_index = jnp.arange(rows, dtype=jnp.int32)
    image_of = row_index // per_image
    picked = image_of[:, None] == jnp.arange(images, dtype=jnp.int32)[None, :]
    count_of = jnp.sum(jnp.where(picked, counts[None, :], 0), axis=1)
    valid = (4 * (row_index % per_image) < count_of).astype(jnp.float32)
    masked = (projected.astype(jnp.float32) * valid[:, None]).astype(jnp.bfloat16)
    owner = owners[:, 0]
    hits = (owner[:, None] == jnp.arange(replicas, dtype=jnp.int32)[None, :]).astype(jnp.int32)
    before = jnp.cumsum(hits, axis=0) - hits
    slot_index = jnp.sum(before * hits, axis=1)
    target = owner * slots + slot_index
    placer = (jnp.arange(replicas * slots, dtype=jnp.int32)[:, None] == target[None, :]).astype(
        jnp.bfloat16
    )
    outgoing = jnp.dot(placer, masked, preferred_element_type=jnp.float32).astype(jnp.bfloat16)
    outgoing = outgoing.reshape(replicas, slots, columns)
    received = lax.all_to_all(outgoing, "dp", split_axis=0, concat_axis=0, tiled=True)
    values = received.astype(jnp.float32)
    square_sums = lax.psum(jnp.sum(values * values, axis=2), ("group", "section", "tensor"))
    scale = lax.rsqrt(square_sums / D + 1e-05)
    normed = (values * scale[:, :, None] * norm_gain[None, None, :]).astype(jnp.bfloat16)
    embedded = normed[None]
    grad_in = cotangent[0].astype(jnp.float32) * norm_gain[None, None, :]
    inner_sums = lax.psum(jnp.sum(grad_in * values, axis=2), ("group", "section", "tensor"))
    inner = inner_sums / D
    slot_grad = (scale[:, :, None] * grad_in - values * (scale**3 * inner)[:, :, None]).astype(
        jnp.bfloat16
    )
    returned = lax.all_to_all(slot_grad, "dp", split_axis=0, concat_axis=0, tiled=True)
    returned = returned.reshape(replicas * slots, columns)
    gathered = lax.dot_general(
        placer, returned, (((0,), (0,)), ((), ())), preferred_element_type=jnp.float32
    )
    back = (gathered * valid[:, None]).astype(jnp.bfloat16)
    input_terms = lax.dot_general(
        back, w_merge, (((1,), (1,)), ((), ())), preferred_element_type=jnp.float32
    )
    grad_merged = lax.psum_scatter(
        input_terms, ("group", "section", "tensor"), scatter_dimension=1, tiled=True
    )
    column_block = lax.all_to_all(merged, "dp", split_axis=1, concat_axis=0, tiled=True)
    grad_weight = lax.dot_general(
        column_block,
        lax.all_gather(back, "dp", axis=0, tiled=True),
        (((0,), (0,)), ((), ())),
        preferred_element_type=jnp.float32,
    )
    return (embedded, grad_merged, grad_weight)


def solution(mesh):
    placed = (
        P("dp", None),
        P("dp"),
        P("dp", None),
        P(None, ("group", "section", "tensor")),
        P(("group", "section", "tensor")),
        P("dp", None, None, ("group", "section", "tensor")),
    )
    return jax.shard_map(
        on_device,
        mesh=mesh,
        in_specs=placed,
        out_specs=(
            P("dp", None, None, ("group", "section", "tensor")),
            P("dp", ("group", "section", "tensor")),
            P("dp", ("group", "section", "tensor")),
        ),
        check_vma=False,
    )
```

profile of v0, /device:TPU:0, one launch (start us, length us, event | category | flops | bytes accessed | tf_op | source)
XLA Modules:
  0.0 182.4 jit_solution(6930971145670902794)
XLA Ops:
  8.0 0.0 all-gather.2.cloned.1.call-start
  8.1 0.7 iota_compare_fusion.3
  8.7 0.7 fusion.18
  9.5 1.2 reduce-window.6
  10.8 0.1 slice.12
  10.8 0.1 copy.23
  11.0 0.1 copy.24
  11.1 0.1 add_bitcast_fusion
  11.2 0.7 fusion.16
  11.9 0.7 multiply_add_fusion
  12.5 0.0 copy-start.2
  12.5 7.0 %convolution_convert_fusion = bf16[384,1024]{1,0:T(8,128)(2,1)S(1)} fusion(bf16[192,5120]{1,0:T(8,128)(2,1)} %param.6, bf16[5120,1024]{1,0:T(8,128)(2,1)} %param.9, f32[192]{0:T(256)S(1)} %compare_convert_fusion, s32[192]{0:T(256)S(1)} %multiply_add_fusion), kind=kOutput, calls=%fused_computation.14 | convolution fusion | flops 2165514240 | bytes 13239808 | tf_op jit(solution)/shard_map/dot_general | solution.py:31
  19.6 0.0 copy-start
  19.6 26.4 %all_to_all.29 = bf16[4,96,1024]{2,1,0:T(8,128)(2,1)S(1)} all-to-all(bf16[4,96,1024]{2,1,0:T(8,128)(2,1)S(1)} %bitcast.38), channel_id=1, replica_groups=mesh['group'=2,'dp'=4,'section'=2,'tensor'=2] {'dp'}, dimensions={0} | all-to-all | bytes 1572864 | tf_op jit(solution)/shard_map/all_to_all | solution.py:33
  46.0 0.0 copy-done.2
  46.0 0.0 copy-done
  46.0 0.4 fusion.3
  46.4 14.3 %all-reduce.1 = (f32[4,96]{1,0:T(4,128)S(1)}, f32[4,96]{1,0:T(4,128)S(1)}) all-reduce(f32[4,96]{1,0:T(4,128)S(1)} %get-tuple-element.19, f32[4,96]{1,0:T(4,128)S(1)} %get-tuple-element.18), channel_id=1, replica_groups=mesh['group'=2,'dp'=4,'section'=2,'tensor'=2] {'group','section','tensor'}, use_global_device_ids=true, to_apply=%region_5.6 | all-reduce | flops 768 | bytes 6144 | tf_op jit(solution)/shard_map/psum | solution.py:35
  60.7 1.4 fusion.5
  62.1 23.6 %all_to_all.30 = bf16[4,96,1024]{2,1,0:T(8,128)(2,1)S(1)} all-to-all(bf16[4,96,1024]{2,1,0:T(8,128)(2,1)S(1)} %get-tuple-element.22), channel_id=1, replica_groups=mesh['group'=2,'dp'=4,'section'=2,'tensor'=2] {'dp'}, dimensions={0} | all-to-all | bytes 1572864 | tf_op jit(solution)/shard_map/all_to_all | solution.py:45
  85.7 1.2 fusion.7
  86.9 0.0 all-gather.2.cloned.1.call-update
  86.9 0.0 reduce-scatter.2.cloned.1.call-start
  86.9 9.7 %fusion.21 = f32[192,5120]{1,0:T(8,128)} fusion(bf16[192,1024]{1,0:T(8,128)(2,1)} %fusion.7, bf16[5120,1024]{1,0:T(8,128)(2,1)} %param.9), kind=kOutput, calls=%fused_computation.48 | convolution fusion | flops 2013265920 | bytes 14811136 | tf_op jit(solution)/shard_map/dot_general | solution.py:51
  96.7 0.0 reduce-scatter.2.cloned.1.call-update
  96.7 1.5 copy-done.1
  98.2 0.1 copy.31
  98.3 64.7 %all_to_all.31 = bf16[192,4,1280]{2,0,1:T(8,128)(2,1)S(1)} all-to-all(bf16[192,4,1280]{2,0,1:T(8,128)(2,1)S(1)} %bitcast.34), channel_id=1, replica_groups=mesh['group'=2,'dp'=4,'section'=2,'tensor'=2] {'dp'}, dimensions={1} | all-to-all | bytes 3932160 | tf_op jit(solution)/shard_map/all_to_all | solution.py:57
  163.1 0.0 all-gather.2.cloned.1.call-done
  163.1 6.0 %convolution_bitcast_fusion = f32[1280,1024]{0,1:T(8,128)} fusion(bf16[768,1024]{1,0:T(8,128)(2,1)} %all-gather.2.cloned.1.call-done, bf16[768,1280]{1,0:T(8,128)(2,1)S(1)} %bitcast.37), kind=kOutput, calls=%fused_computation | convolution fusion | flops 2013265920 | bytes 8781824 | tf_op jit(solution)/shard_map/dot_general | solution.py:58
  169.1 5.9 %copy.26 = f32[1280,1024]{1,0:T(8,128)} copy(f32[1280,1024]{0,1:T(8,128)} %convolution_bitcast_fusion) | data formatting | bytes 10485760
  174.9 0.0 reduce-scatter.2.cloned.1.call-done
  (9 shorter events, 0.1 us)
Async XLA Ops:
  8.0 155.1 %all-gather.2.cloned.1.call-start = ((), (), s32[]{:S(2)}) async-start(), calls=%async_computation.5 | async-start | bytes 1966080 | tf_op jit(solution)/shard_map/all_gather | solution.py:60
  12.5 33.4 %copy-start.2 = (f32[1024]{0:T(1024)S(1)}, f32[1024]{0:T(1024)}, u32[]{:S(2)}) copy-start(f32[1024]{0:T(1024)} %param.10) | copy-start | bytes 12292
  19.6 26.4 %copy-start = (bf16[1,4,96,1024]{3,2,1,0:T(8,128)(2,1)S(1)}, bf16[1,4,96,1024]{3,2,1,0:T(8,128)(2,1)}, u32[]{:S(2)}) copy-start(bf16[1,4,96,1024]{3,2,1,0:T(8,128)(2,1)} %param.11) | copy-start | bytes 2359300
  86.9 88.1 %reduce-scatter.2.cloned.1.call-start = ((), (), s32[]{:S(2)}) async-start(), calls=%async_computation.4 | async-start | bytes 4423680 | tf_op jit(solution)/shard_map/reduce_scatter | solution.py:54
  96.7 1.5 copy-start.1
Sparse Core Ops, SparseCore 0:
  87.0 58.4 all-gather.1
Sparse Core Ops, SparseCore 1:
  96.8 46.7 reduce-scatter.1
where the time goes:
time: 183 us; the launch traced here: 182 us
  blocking collectives  129 us (70%)
  matrix products  23.9 us (13%)
  between operations  15.5 us (8%)
  local copies, waits for them, and re-layouts  7.84 us (4%)
  other arithmetic  6.04 us (3%)
    all_to_all x1, blocking collectives, on_device(): lax.all_to_all(merged, 'dp', split_axis=1, concat_axis=0, tiled=True)  64.7 us
    all_to_all x1, blocking collectives, on_device(): lax.all_to_all(outgoing, 'dp', split_axis=0, concat_axis=0, tiled=True)  26.4 us
    all_to_all x1, blocking collectives, on_device(): lax.all_to_all(slot_grad, 'dp', split_axis=0, concat_axis=0, tiled=True)  23.6 us
    psum x1, blocking collectives, on_device(): lax.psum(jnp.sum(values * values, axis=2), ('group', 'section', 'tensor'))  14.3 us
    dot_general x1, matrix products, on_device(): lax.dot_general(back, w_merge, (((1,), (1,)), ((), ())), preferred_elemen...  9.72 us
    unnamed x8, local copies, waits for them, and re-layouts  7.42 us
    dot_general x1, matrix products, on_device(): jnp.dot(placer, masked, preferred_element_type=jnp.float32)  7.02 us
    dot_general x1, matrix products, on_device(): lax.dot_general(column_block, lax.all_gather(back, 'dp', axis=0, tiled=Tr...  5.97 us
  transfers between devices with their start and end apart: 2, of which 0 were waited for; matrix products, arithmetic and copies ran while one was open for 12% of the time, Pallas kernels for 0%

commit v1 on v0

--- a/solution.py
+++ b/solution.py
@@ -32,7 +32,11 @@
     outgoing = outgoing.reshape(replicas, slots, columns)
     received = lax.all_to_all(outgoing, "dp", split_axis=0, concat_axis=0, tiled=True)
     values = received.astype(jnp.float32)
-    square_sums = lax.psum(jnp.sum(values * values, axis=2), ("group", "section", "tensor"))
+
+    def zones_manage(unit, a_name):
+        return lax.all_gather(unit, axis_name=a_name).sum(axis=0)
+
+    square_sums = zones_manage(jnp.sum(values * values, axis=2), ("group", "section", "tensor"))
     scale = lax.rsqrt(square_sums / D + 1e-05)
     normed = (values * scale[:, :, None] * norm_gain[None, None, :]).astype(jnp.bfloat16)
     embedded = normed[None]

time: 183 us -> 203 us (1.11)
  blocking collectives: 129 us -> 149 us
    all_gather x0 -> x1, blocking collectives: none -> 19.9 us  [zones_manage(): return lax.all_gather(unit, axis_name=a_name).sum(axis=0)]
  transfers between devices with their start and end apart: 2 -> 2, of which waited for: 0 -> 0; matrix products, arithmetic and copies ran while one was open for 12% -> 11% of each run, Pallas kernels for 0% -> 0%
where the time goes in v1:
time: 203 us
  blocking collectives  149 us (73%)
  matrix products  23.9 us (12%)
  between operations  15.5 us (8%)
  local copies, waits for them, and re-layouts  7.84 us (4%)
  other arithmetic  6.06 us (3%)
    all_to_all x1, blocking collectives, on_device(): lax.all_to_all(merged, 'dp', split_axis=1, concat_axis=0, tiled=True)  64.7 us
    all_to_all x1, blocking collectives, on_device(): lax.all_to_all(outgoing, 'dp', split_axis=0, concat_axis=0, tiled=True)  26.4 us
    all_to_all x1, blocking collectives, on_device(): lax.all_to_all(slot_grad, 'dp', split_axis=0, concat_axis=0, tiled=True)  24 us
    all_gather x1, blocking collectives, zones_manage(): return lax.all_gather(unit, axis_name=a_name).sum(axis=0)  19.9 us
    psum x1, blocking collectives, on_device(): lax.psum(jnp.sum(grad_in * values, axis=2), ('group', 'section', 'tensor'))  14.3 us
    dot_general x1, matrix products, on_device(): lax.dot_general(back, w_merge, (((1,), (1,)), ((), ())), preferred_elemen...  9.73 us
    unnamed x8, local copies, waits for them, and re-layouts  7.42 us
    dot_general x1, matrix products, on_device(): jnp.dot(placer, masked, preferred_element_type=jnp.float32)  7.02 us
  transfers between devices with their start and end apart: 2, of which 0 were waited for; matrix products, arithmetic and copies ran while one was open for 11% of the time, Pallas kernels for 0%

profile of v1, /device:TPU:0, one launch (start us, length us, event | category | flops | bytes accessed | tf_op | source)
XLA Modules:
  0.0 202.6 jit_solution(12734765205774224603)
XLA Ops:
  8.0 0.0 all-gather.4.cloned.1.call-start
  8.1 0.7 iota_compare_fusion.3
  8.7 0.7 fusion.18
  9.5 1.2 reduce-window.6
  10.8 0.1 slice.12
  10.8 0.1 copy.23
  11.0 0.1 copy.24
  11.1 0.1 add_bitcast_fusion
  11.2 0.7 fusion.16
  11.9 0.7 multiply_add_fusion
  12.5 0.0 copy-start.2
  12.5 7.0 %convolution_convert_fusion = bf16[384,1024]{1,0:T(8,128)(2,1)S(1)} fusion(bf16[192,5120]{1,0:T(8,128)(2,1)} %param.6, bf16[5120,1024]{1,0:T(8,128)(2,1)} %param.9, f32[192]{0:T(256)S(1)} %compare_convert_fusion, s32[192]{0:T(256)S(1)} %multiply_add_fusion), kind=kOutput, calls=%fused_computation.14 | convolution fusion | flops 2165514240 | bytes 13239808 | tf_op jit(solution)/shard_map/dot_general | solution.py:31
  19.6 0.0 copy-start
  19.6 26.4 %all_to_all.29 = bf16[4,96,1024]{2,1,0:T(8,128)(2,1)S(1)} all-to-all(bf16[4,96,1024]{2,1,0:T(8,128)(2,1)S(1)} %bitcast.39), channel_id=1, replica_groups=mesh['group'=2,'dp'=4,'section'=2,'tensor'=2] {'dp'}, dimensions={0} | all-to-all | bytes 1572864 | tf_op jit(solution)/shard_map/all_to_all | solution.py:33
  46.0 0.0 copy-done.2
  46.0 0.0 copy-done
  46.0 0.4 fusion.3
  46.4 14.3 %psum.7 = f32[4,96]{1,0:T(4,128)S(1)} all-reduce(f32[4,96]{1,0:T(4,128)S(1)} %get-tuple-element.18), channel_id=1, replica_groups=mesh['group'=2,'dp'=4,'section'=2,'tensor'=2] {'group','section','tensor'}, use_global_device_ids=true, to_apply=%region_7.8 | all-reduce | flops 384 | bytes 3072 | tf_op jit(solution)/shard_map/psum | solution.py:44
  60.7 19.9 %all-gather.1 = f32[8,4,96]{2,1,0:T(4,128)S(1)} all-gather(f32[1,4,96]{2,1,0:T(4,128)S(1)} %bitcast.44), channel_id=2, replica_groups=mesh['group'=2,'dp'=4,'section'=2,'tensor'=2] {'group','section','tensor'}, dimensions={0}, use_global_device_ids=true | all-gather | bytes 13824 | tf_op jit(solution)/shard_map/all_gather | solution.py:37
  80.6 1.4 fusion.5
  82.0 24.0 %all_to_all.30 = bf16[4,96,1024]{2,1,0:T(8,128)(2,1)S(1)} all-to-all(bf16[4,96,1024]{2,1,0:T(8,128)(2,1)S(1)} %get-tuple-element.20), channel_id=1, replica_groups=mesh['group'=2,'dp'=4,'section'=2,'tensor'=2] {'dp'}, dimensions={0} | all-to-all | bytes 1572864 | tf_op jit(solution)/shard_map/all_to_all | solution.py:49
  105.9 1.2 fusion.7
  107.1 0.0 all-gather.4.cloned.1.call-update
  107.1 0.0 reduce-scatter.2.cloned.1.call-start
  107.2 9.7 %fusion.21 = f32[192,5120]{1,0:T(8,128)} fusion(bf16[192,1024]{1,0:T(8,128)(2,1)} %fusion.7, bf16[5120,1024]{1,0:T(8,128)(2,1)} %param.9), kind=kOutput, calls=%fused_computation.48 | convolution fusion | flops 2013265920 | bytes 14811136 | tf_op jit(solution)/shard_map/dot_general | solution.py:55
  116.9 0.0 copy-start.1
  116.9 0.0 reduce-scatter.2.cloned.1.call-update
  116.9 1.5 copy-done.1
  118.5 0.1 copy.31
  118.6 64.7 %all_to_all.31 = bf16[192,4,1280]{2,0,1:T(8,128)(2,1)S(1)} all-to-all(bf16[192,4,1280]{2,0,1:T(8,128)(2,1)S(1)} %bitcast.35), channel_id=1, replica_groups=mesh['group'=2,'dp'=4,'section'=2,'tensor'=2] {'dp'}, dimensions={1} | all-to-all | bytes 3932160 | tf_op jit(solution)/shard_map/all_to_all | solution.py:61
  183.3 6.0 %convolution_bitcast_fusion = f32[1280,1024]{0,1:T(8,128)} fusion(bf16[768,1024]{1,0:T(8,128)(2,1)} %all-gather.4.cloned.1.call-done, bf16[768,1280]{1,0:T(8,128)(2,1)S(1)} %bitcast.38), kind=kOutput, calls=%fused_computation | convolution fusion | flops 2013265920 | bytes 8781824 | tf_op jit(solution)/shard_map/dot_general | solution.py:62
  189.2 5.9 %copy.26 = f32[1280,1024]{1,0:T(8,128)} copy(f32[1280,1024]{0,1:T(8,128)} %convolution_bitcast_fusion) | data formatting | bytes 10485760
  (11 shorter events, 0.1 us)
Async XLA Ops:
  8.0 175.3 %all-gather.4.cloned.1.call-start = ((), (), s32[]{:S(2)}) async-start(), calls=%async_computation.5 | async-start | bytes 1966080 | tf_op jit(solution)/shard_map/all_gather | solution.py:64
  12.5 33.4 %copy-start.2 = (f32[1024]{0:T(1024)S(1)}, f32[1024]{0:T(1024)}, u32[]{:S(2)}) copy-start(f32[1024]{0:T(1024)} %param.10) | copy-start | bytes 12292
  19.6 26.4 %copy-start = (bf16[1,4,96,1024]{3,2,1,0:T(8,128)(2,1)S(1)}, bf16[1,4,96,1024]{3,2,1,0:T(8,128)(2,1)}, u32[]{:S(2)}) copy-start(bf16[1,4,96,1024]{3,2,1,0:T(8,128)(2,1)} %param.11) | copy-start | bytes 2359300
  107.1 88.0 %reduce-scatter.2.cloned.1.call-start = ((), (), s32[]{:S(2)}) async-start(), calls=%async_computation.4 | async-start | bytes 4423680 | tf_op jit(solution)/shard_map/reduce_scatter | solution.py:58
  116.9 1.6 copy-start.1
Sparse Core Ops, SparseCore 0:
  107.3 57.0 all-gather.3
Sparse Core Ops, SparseCore 1:
  117.0 46.6 reduce-scatter.1
